TPU v7x, 32 devices: a whole 2x2x4 slice. The times are simulated.
32 devices in a mesh: lon: 8 (over y, x, core), lat: 4 (over z).
Axes of the slice: x: 2, y: 2, z: 4, core: 2. Of those that a mesh axis runs over, the one named last changes fastest.
Arguments:
- ensemble: float32 [8, 4, 80, 32, 256], P('lon', 'lat'), may hold values from -6 to 6
- obs_block: int32 [3, 128], replicated, may hold values from 0 to 31, as said below
- obs_column: int32 [3, 128], replicated, may hold values from 0 to 255
- obs_value: float32 [3, 128], replicated, may hold values from -8 to 8
- obs_error: float32 [3, 128], replicated, may hold values from 0.5 to 2
- loc_mask: int32 [8, 4, 3, 128, 256], P('lon', 'lat'), may hold values from 0 to 1, as said below
Outputs:
- analysis: float32 [8, 4, 80, 32, 256], P('lon', 'lat')
Inputs may be any that keep to these rules, and one draw needn't show every extreme that they name: `obs_block`: observations fall more often on blocks of low index. `loc_mask`: an observation may update only columns of its own block and of blocks at most two blocks away along longitude (cyclically) and latitude; all other blocks have zeros for it.
All inputs are finite; a program needn't handle non-finite values.
Results may differ from a plain program's by a relative error of at most 0.0001.
Values sent between devices are 32-bit elements; how exact they have to be, the bound alone decides.
No kernel may reach another device: no remote copies, remote signals or barrier semaphores. Data moves between devices by JAX's collectives and lax.ppermute only.
A program may use at most 64 MiB of HBM per device.

v0:
```python
import jax
import jax.numpy as jnp
from jax import lax
from jax.sharding import PartitionSpec as P


def solve_rows(whitened, innov_raw):
    count = whitened.shape[0]
    cmat = jnp.eye(count, dtype=jnp.float32) + jnp.dot(
        whitened, whitened.T, precision=lax.Precision.HIGHEST
    )
    chol = jnp.linalg.cholesky(cmat)
    gain_rows = jax.scipy.linalg.cho_solve((chol, True), whitened)
    innov = jax.scipy.linalg.cho_solve((chol, True), innov_raw)
    return (gain_rows, innov)


def body(ensemble, obs_block, obs_column, obs_value, obs_error, loc_mask):
    members = ensemble.shape[2]
    levels = ensemble.shape[3]
    columns = ensemble.shape[4]
    count = obs_block.shape[1]
    scale = 1.0 / jnp.sqrt(jnp.float32(members - 1))
    n_lat = lax.axis_size("lat")
    lat_here = lax.axis_index("lat")
    state = ensemble.reshape(members, levels * columns)
    col_ids = jnp.arange(columns, dtype=jnp.int32)
    for batch in range(obs_block.shape[0]):
        blocks = obs_block[batch]
        pick = obs_column[batch][:, None] == col_ids[None, :]
        surface = state[:, :columns]
        piece = lax.all_gather(surface[None], "lon", axis=0, tiled=True)
        width = piece.shape[0]
        ids = jnp.arange(width, dtype=jnp.int32) * n_lat + lat_here
        select = ((blocks[:, None] == ids[None, :])[:, :, None] & pick[:, None, :]).astype(
            jnp.float32
        )
        row_part = jnp.zeros((count, members), jnp.float32) + jnp.einsum(
            "pkc,kmc->pm", select, piece, precision=lax.Precision.HIGHEST
        )
        obs_ens = lax.psum(row_part, "lat")
        obs_mean = jnp.mean(obs_ens, axis=1)
        errors = obs_error[batch]
        whitened = (obs_ens - obs_mean[:, None]) * scale / errors[:, None]
        innov_raw = (obs_value[batch] - obs_mean) / errors
        gain_rows, innov = solve_rows(whitened, innov_raw)
        coef = jnp.concatenate([-0.5 * gain_rows.T, (innov * scale)[None, :]], axis=0)
        weights = loc_mask[0, 0, batch].astype(jnp.float32)
        mean = jnp.mean(state, axis=0)
        pert = state - mean[None, :]
        proj = jnp.dot(whitened, pert, precision=lax.Precision.HIGHEST)
        proj = (proj.reshape(count, levels, columns) * weights[:, None, :]).reshape(
            count, levels * columns
        )
        incr = jnp.dot(coef, proj, precision=lax.Precision.HIGHEST)
        state = pert + incr[:members] + (mean + incr[members])[None, :]
    return state.reshape(ensemble.shape)


def solution(mesh):
    placed = (
        P("lon", "lat", None, None, None),
        P(),
        P(),
        P(),
        P(),
        P("lon", "lat", None, None, None),
    )
    return jax.shard_map(
        body,
        mesh=mesh,
        in_specs=placed,
        out_specs=P("lon", "lat", None, None, None),
        check_vma=False,
    )
```

profile of v0, /device:TPU:0, one launch (start us, length us, event | category | flops | bytes accessed | tf_op | source)
XLA Modules:
  0.0 211.4 jit_solution(10639633567476785206)
XLA Ops:
  0.0 0.8 slice_bitcast_fusion.2
  0.9 3.4 %copy.32 = f32[10,8,32,256]{3,1,2,0:T(8,128)S(1)} copy(f32[10,8,32,256]{3,2,1,0:T(8,128)} %bitcast.215) | data formatting | bytes 5242880
  4.3 11.6 %all-gather = f32[640,256]{1,0:T(8,128)S(1)} all-gather(f32[80,256]{1,0:T(8,128)S(1)} %slice.116), channel_id=2, replica_groups=mesh['lon'=8,'lat'=4] {'lon'}, dimensions={0}, use_global_device_ids=true | all-gather | bytes 737280 | tf_op jit(solution)/shard_map/all_gather | solution.py:32
  16.0 0.7 convolution_bitcast_fusion.2
  16.8 19.8 %psum.21 = f32[128,80]{0,1:T(8,128)S(1)} all-reduce(f32[128,80]{0,1:T(8,128)S(1)} %convolution_bitcast_fusion.2), channel_id=1, replica_groups=mesh['lon'=8,'lat'=4] {'lat'}, use_global_device_ids=true, to_apply=%region_1.0 | all-reduce | flops 10240 | bytes 81920 | tf_op jit(solution)/shard_map/psum | solution.py:41
  36.7 0.3 convolution_add_fusion.2
  37.1 11.7 %cholesky.59 = f32[128,128]{1,0:T(8,128)S(1)} custom-call(f32[128,128]{1,0:T(8,128)S(1)} %fusion.63), custom_call_target="Cholesky" | custom-call | tf_op jit(solution)/shard_map/jit(cholesky)/cholesky | solution.py:12
  48.8 0.6 compare_reduce_fusion.2
  49.5 0.7 fusion.31
  50.1 9.8 %custom-call.16 = f32[1,128,128]{1,2,0:T(8,128)S(1)} custom-call(f32[1,128,128]{2,1,0:T(8,128)S(1)} %fusion.31), custom_call_target="InvertDiagBlocksLowerTriangular" | custom-call | tf_op jit(solution)/shard_map/jit(_cho_solve)/triangular_solve | solution.py:13
  59.9 0.3 fusion.61
  61.0 1.9 reduce_sum.54
  62.9 0.3 broadcast_subtract_fusion
  63.2 0.7 copy-done.2
  64.0 5.1 %fusion.8 = f32[128,32,256]{2,0,1:T(8,128)} fusion(f32[10,32,8,256]{3,2,1,0:T(8,128)S(1)} %bitcast.216, f32[128,256]{1,0:T(8,128)S(1)} %get-tuple-element.13, f32[128,80]{0,1:T(8,128)S(1)} %psum.21, f32[128]{0:T(128)S(1)} %get-tuple-element.18, f32[128]{0:T(128)S(1)} %broadcast_multiply_fusion.4), kind=kOutput, calls=%fused_computation.13 | convolution fusion | flops 1007712256 | bytes 6988800 | tf_op jit(solution)/shard_map/dot_general | solution.py:51
  69.1 5.6 %copy.21 = f32[128,32,256]{0,2,1:T(8,128)} copy(f32[128,32,256]{2,0,1:T(8,128)} %fusion.8) | data formatting | bytes 8388608 | tf_op jit(solution)/shard_map/mul | solution.py:52
  74.7 5.9 %fusion.34 = f32[81,8192]{1,0:T(8,128)S(1)} fusion(f32[128,8192]{0,1:T(8,128)} %bitcast.210, f32[1,128]{0,1:T(8,128)S(1)} %copy.19, f32[80,128]{0,1:T(8,128)S(1)} %fusion.15), kind=kOutput, calls=%fused_computation.62 | convolution fusion | flops 1019226240 | bytes 6889984 | tf_op jit(solution)/shard_map/dot_general | solution.py:55
  80.7 0.5 fusion.82
  81.2 1.5 copy-done
  82.6 10.1 %all-gather.1 = f32[640,256]{1,0:T(8,128)S(1)} all-gather(f32[80,256]{1,0:T(8,128)S(1)} %slice.119), channel_id=3, replica_groups=mesh['lon'=8,'lat'=4] {'lon'}, dimensions={0}, use_global_device_ids=true | all-gather | bytes 737280 | tf_op jit(solution)/shard_map/all_gather | solution.py:32
  92.8 0.7 convolution_bitcast_fusion.1
  93.6 16.3 %psum.22 = f32[128,80]{0,1:T(8,128)S(1)} all-reduce(f32[128,80]{0,1:T(8,128)S(1)} %convolution_bitcast_fusion.1), channel_id=1, replica_groups=mesh['lon'=8,'lat'=4] {'lat'}, use_global_device_ids=true, to_apply=%region_6.0 | all-reduce | flops 10240 | bytes 81920 | tf_op jit(solution)/shard_map/psum | solution.py:41
  109.9 0.3 convolution_add_fusion.1
  110.3 11.7 %cholesky.70 = f32[128,128]{1,0:T(8,128)S(1)} custom-call(f32[128,128]{1,0:T(8,128)S(1)} %fusion.57), custom_call_target="Cholesky" | custom-call | tf_op jit(solution)/shard_map/jit(cholesky)/cholesky | solution.py:12
  122.1 0.7 compare_reduce_fusion.1
  122.8 0.7 fusion.32
  123.5 9.8 %custom-call.18 = f32[1,128,128]{1,2,0:T(8,128)S(1)} custom-call(f32[1,128,128]{2,1,0:T(8,128)S(1)} %fusion.32), custom_call_target="InvertDiagBlocksLowerTriangular" | custom-call | tf_op jit(solution)/shard_map/jit(_cho_solve)/triangular_solve | solution.py:13
  133.3 0.3 fusion.55
  134.4 0.3 mul.86
  134.7 3.3 %copy.35 = f32[16,8,32,256]{3,1,2,0:T(8,128)S(1)} copy(f32[16,8,32,256]{3,2,1,0:T(8,128)S(1)} %bitcast.213) | data formatting | bytes 8388608
  138.1 4.0 %convolution_multiply_fusion.1 = f32[128,8192]{1,0:T(8,128)S(1)} fusion(f32[128,8192]{1,0:T(8,128)S(1)} %bitcast.211, f32[80,8192]{1,0:T(8,128)S(1)} %copy-done.1, f32[8192]{0:T(1024)S(1)} %broadcast_multiply_fusion.1, f32[128,80]{0,1:T(8,128)S(1)} %psum.22, f32[128]{0:T(128)S(1)} %get-tuple-element.19, f32[128]{0:T(128)S(1)} %broadcast_multiply_fusion.3), kind=kOutput, calls=%fused_computation.1 | convolution fusion | flops 1008367616 | bytes 11084800 | tf_op jit(solution)/shard_map/dot_general | solution.py:51
  142.0 3.0 %fusion.38 = f32[81,8192]{1,0:T(8,128)S(1)} fusion(f32[128,8192]{1,0:T(8,128)S(1)} %convolution_multiply_fusion.1, f32[1,128]{0,1:T(8,128)S(1)} %copy.24, f32[80,128]{0,1:T(8,128)S(1)} %fusion.14), kind=kOutput, calls=%fused_computation.66 | convolution fusion | flops 1019226240 | bytes 6889984 | tf_op jit(solution)/shard_map/dot_general | solution.py:55
  145.1 0.5 fusion.80
  145.6 9.2 %all-gather.2 = f32[640,256]{1,0:T(8,128)S(1)} all-gather(f32[80,256]{1,0:T(8,128)S(1)} %slice.122), channel_id=4, replica_groups=mesh['lon'=8,'lat'=4] {'lon'}, dimensions={0}, use_global_device_ids=true | all-gather | bytes 737280 | tf_op jit(solution)/shard_map/all_gather | solution.py:32
  154.8 0.7 convolution_bitcast_fusion
  155.6 18.1 %psum.23 = f32[128,80]{0,1:T(8,128)S(1)} all-reduce(f32[128,80]{0,1:T(8,128)S(1)} %convolution_bitcast_fusion), channel_id=1, replica_groups=mesh['lon'=8,'lat'=4] {'lat'}, use_global_device_ids=true, to_apply=%region_9.13 | all-reduce | flops 10240 | bytes 81920 | tf_op jit(solution)/shard_map/psum | solution.py:41
  173.8 0.3 convolution_add_fusion
  174.2 11.7 %cholesky.81 = f32[128,128]{1,0:T(8,128)S(1)} custom-call(f32[128,128]{1,0:T(8,128)S(1)} %fusion.51), custom_call_target="Cholesky" | custom-call | tf_op jit(solution)/shard_map/jit(cholesky)/cholesky | solution.py:12
  185.9 0.6 compare_reduce_fusion
  186.6 0.7 fusion.33
  187.2 9.8 %custom-call.20 = f32[1,128,128]{1,2,0:T(8,128)S(1)} custom-call(f32[1,128,128]{2,1,0:T(8,128)S(1)} %fusion.33), custom_call_target="InvertDiagBlocksLowerTriangular" | custom-call | tf_op jit(solution)/shard_map/jit(_cho_solve)/triangular_solve | solution.py:13
  197.1 0.3 fusion.49
  198.1 0.3 mul.93
  198.4 3.3 %copy.36 = f32[16,8,32,256]{3,1,2,0:T(8,128)S(1)} copy(f32[16,8,32,256]{3,2,1,0:T(8,128)S(1)} %bitcast.214) | data formatting | bytes 8388608
  201.7 3.8 %convolution_multiply_fusion = f32[128,8192]{1,0:T(8,128)S(1)} fusion(f32[128,8192]{1,0:T(8,128)S(1)} %bitcast.212, f32[80,8192]{1,0:T(8,128)S(1)} %get-tuple-element.8, f32[8192]{0:T(1024)S(1)} %broadcast_multiply_fusion, f32[128,80]{0,1:T(8,128)S(1)} %psum.23, f32[128]{0:T(128)S(1)} %get-tuple-element.17, f32[128]{0:T(128)S(1)} %broadcast_multiply_fusion.2), kind=kOutput, calls=%fused_computation | convolution fusion | flops 1008367616 | bytes 11084800 | tf_op jit(solution)/shard_map/dot_general | solution.py:51
  205.5 3.0 %fusion.42 = f32[81,8192]{1,0:T(8,128)S(1)} fusion(f32[128,8192]{1,0:T(8,128)S(1)} %convolution_multiply_fusion, f32[1,128]{0,1:T(8,128)S(1)} %copy.27, f32[80,128]{0,1:T(8,128)S(1)} %fusion.13), kind=kOutput, calls=%fused_computation.70 | convolution fusion | flops 1019226240 | bytes 6889984 | tf_op jit(solution)/shard_map/dot_general | solution.py:55
  208.6 0.3 fusion.3
  208.9 2.3 %copy.37 = f32[10,8,32,256]{3,2,1,0:T(8,128)} copy(f32[10,8,32,256]{3,1,2,0:T(8,128)S(1)} %bitcast.217) | data formatting | bytes 5242880
  (56 shorter events, 3.2 us)
Async XLA Ops:
  0.9 15.1 %copy-start.5 = (s32[3,128]{1,0:T(4,128)S(1)}, s32[3,128]{1,0:T(4,128)}, u32[]{:S(2)}) copy-start(s32[3,128]{1,0:T(4,128)} %param.13) | copy-start | bytes 4612
  0.9 35.8 %copy-start.3 = (f32[3,128]{1,0:T(4,128)S(1)}, f32[3,128]{1,0:T(4,128)}, u32[]{:S(2)}) copy-start(f32[3,128]{1,0:T(4,128)} %param.15) | copy-start | bytes 4612
  4.3 56.2 %copy-start.4 = (f32[3,128]{1,0:T(4,128)S(1)}, f32[3,128]{1,0:T(4,128)}, u32[]{:S(2)}) copy-start(f32[3,128]{1,0:T(4,128)} %param.14) | copy-start | bytes 4612
  62.9 1.0 copy-start.2
  81.1 1.5 copy-start
  134.7 3.4 %copy-start.1 = (f32[80,8192]{1,0:T(8,128)S(1)}, f32[80,8192]{1,0:T(8,128)}, u32[]{:S(2)}) copy-start(f32[80,8192]{1,0:T(8,128)} %copy-done) | copy-start | bytes 7864324
where the time goes:
time: 215 us; the launch traced here: 211 us
  blocking collectives  85.1 us (40%)
  other arithmetic  72.7 us (34%)
  matrix products  30.5 us (14%)
  local copies, waits for them, and re-layouts  22.4 us (10%)
    psum x3, blocking collectives, body(): obs_ens = lax.psum(row_part, 'lat')  54.3 us
    another operation x9, other arithmetic, solve_rows(): chol = jnp.linalg.cholesky(cmat)  37.2 us
    another operation x6, other arithmetic, solve_rows(): gain_rows = jax.scipy.linalg.cho_solve((chol, True), whitened)  31.4 us
    all_gather x3, blocking collectives, body(): piece = lax.all_gather(surface[None], 'lon', axis=0, tiled=True)  30.9 us
    unnamed x18, local copies, waits for them, and re-layouts  14.6 us
    dot_general x3, matrix products, body(): proj = jnp.dot(whitened, pert, precision=lax.Precision.HIGHEST)  12.9 us
    dot_general x3, matrix products, body(): incr = jnp.dot(coef, proj, precision=lax.Precision.HIGHEST)  12 us
    mul x3, local copies, waits for them, and re-layouts, body(): proj.reshape(count, levels, columns) * weights[:, None, :]  6.22 us

commit v1 on v0

--- a/solution.py
+++ b/solution.py
@@ -2,6 +2,18 @@
 import jax.numpy as jnp
 from jax import lax
 from jax.sharding import PartitionSpec as P
+
+
+def collect(array, axis, dim):
+    ways, here = (lax.axis_size(axis), lax.axis_index(axis))
+    grown, reach = (array, 1)
+    while reach < ways:
+        theirs = lax.ppermute(grown, axis, [(d, d ^ reach) for d in range(ways)])
+        mine_first = jnp.concatenate([grown, theirs], axis=dim)
+        theirs_first = jnp.concatenate([theirs, grown], axis=dim)
+        grown = jnp.where(here & reach == 0, mine_first, theirs_first)
+        reach = 2 * reach
+    return grown
 
 
 def solve_rows(whitened, innov_raw):
@@ -29,7 +41,7 @@
         blocks = obs_block[batch]
         pick = obs_column[batch][:, None] == col_ids[None, :]
         surface = state[:, :columns]
-        piece = lax.all_gather(surface[None], "lon", axis=0, tiled=True)
+        piece = collect(surface[None], "lon", 0)
         width = piece.shape[0]
         ids = jnp.arange(width, dtype=jnp.int32) * n_lat + lat_here
         select = ((blocks[:, None] == ids[None, :])[:, :, None] & pick[:, None, :]).astype(

time: 215 us -> 237 us (1.10)
  blocking collectives: 85.1 us -> 55 us
  waiting for transfers between devices: 0 us -> 26.5 us
  starting transfers between devices: 0 us -> 11.3 us
  matrix products: 30.5 us -> 39.1 us
  other arithmetic: 72.7 us -> 76.3 us
  local copies, waits for them, and re-layouts: 22.4 us -> 25 us
    all_gather x3 -> x0, blocking collectives: 30.9 us -> none  [body(): piece = lax.all_gather(surface[None], 'lon', axis=0, tiled=True)]
    ppermute x0 -> x9, waiting for transfers between devices: none -> 26.5 us  [collect(): theirs = lax.ppermute(grown, axis, [(d, d ^ reach) for d in range(ways)])]
    ppermute x0 -> x9, starting transfers between devices: none -> 11.3 us  [collect(): theirs = lax.ppermute(grown, axis, [(d, d ^ reach) for d in range(ways)])]
    dot_general x3, matrix products: 12.9 us -> 18.5 us  [body(): proj = jnp.dot(whitened, pert, precision=lax.Precision.HIGHEST)]
    unnamed x18 -> x38, local copies, waits for them, and re-layouts: 14.6 us -> 16.9 us
  transfers between devices with their start and end apart: 0 -> 9, of which waited for: 0 -> 8; matrix products, arithmetic and copies ran while one was open for 0% -> 8% of each run, Pallas kernels for 0% -> 0%
where the time goes in v1:
time: 237 us; the launch traced here: 234 us
  other arithmetic  76.3 us (32%)
  blocking collectives  55 us (23%)
  matrix products  39.1 us (16%)
  waiting for transfers between devices  26.5 us (11%)
  local copies, waits for them, and re-layouts  25 us (11%)
  starting transfers between devices  11.3 us (5%)
    psum x3, blocking collectives, body(): obs_ens = lax.psum(row_part, 'lat')  55 us
    another operation x9, other arithmetic, solve_rows(): chol = jnp.linalg.cholesky(cmat)  37.3 us
    another operation x6, other arithmetic, solve_rows(): gain_rows = jax.scipy.linalg.cho_solve((chol, True), whitened)  31.4 us
    ppermute x9, waiting for transfers between devices, collect(): theirs = lax.ppermute(grown, axis, [(d, d ^ reach) for d in range(ways)])  26.5 us
    dot_general x3, matrix products, body(): proj = jnp.dot(whitened, pert, precision=lax.Precision.HIGHEST)  18.5 us
    unnamed x38, local copies, waits for them, and re-layouts  16.9 us
    dot_general x3, matrix products, body(): incr = jnp.dot(coef, proj, precision=lax.Precision.HIGHEST)  12.3 us
    ppermute x9, starting transfers between devices, collect(): theirs = lax.ppermute(grown, axis, [(d, d ^ reach) for d in range(ways)])  11.3 us
  transfers between devices with their start and end apart: 9, of which 8 were waited for; matrix products, arithmetic and copies ran while one was open for 8% of the time, Pallas kernels for 0%

profile of v1, /device:TPU:0, one launch (start us, length us, event | category | flops | bytes accessed | tf_op | source)
XLA Modules:
  0.0 233.9 jit_solution(14131003846801823058)
XLA Ops:
  0.0 3.4 %copy.32 = f32[10,8,32,256]{3,1,2,0:T(8,128)S(1)} copy(f32[10,8,32,256]{3,2,1,0:T(8,128)} %bitcast.215) | data formatting | bytes 5242880
  4.6 0.7 iota_compare_fusion.2
  5.3 1.9 reduce_sum.54
  7.2 1.7 broadcast_subtract_fusion
  9.0 2.6 %collective-permute-start.1 = (f32[2,80,256]{2,1,0:T(8,128)S(1)}, f32[2,80,256]{2,1,0:T(8,128)S(1)}, u32[]{:S(2)}, u32[]{:S(2)}) collective-permute-start(f32[2,80,256]{2,1,0:T(8,128)S(1)} %maximum_select_fusion.9), channel_id=1, source_target_pairs={{0,8},{4,12},{8,0},{12,4},{16,24},{20,28},{24,16},{28,20},{1,9},{5... | collective-permute-start | bytes 491528 | tf_op jit(solution)/shard_map/ppermute | solution.py:11
  12.2 4.2 %collective-permute-done.1 = f32[2,80,256]{2,1,0:T(8,128)S(1)} collective-permute-done((f32[2,80,256]{2,1,0:T(8,128)S(1)}, f32[2,80,256]{2,1,0:T(8,128)S(1)}, u32[]{:S(2)}, u32[]{:S(2)}) %collective-permute-start.1) | collective-permute-done | bytes 163872 | tf_op jit(solution)/shard_map/ppermute | solution.py:11
  16.4 0.7 maximum_select_fusion.6
  17.1 1.8 collective-permute-start.2
  20.2 6.8 %collective-permute-done.2 = f32[4,80,256]{2,1,0:T(8,128)} collective-permute-done((f32[4,80,256]{2,1,0:T(8,128)}, f32[4,80,256]{2,1,0:T(8,128)}, u32[]{:S(2)}, u32[]{:S(2)}) %collective-permute-start.2) | collective-permute-done | bytes 327712 | tf_op jit(solution)/shard_map/ppermute | solution.py:11
  27.0 2.0 convolution_bitcast_fusion.2
  29.0 20.2 %psum.21 = f32[128,80]{0,1:T(8,128)S(1)} all-reduce(f32[128,80]{0,1:T(8,128)S(1)} %convolution_bitcast_fusion.2), channel_id=1, replica_groups=mesh['lon'=8,'lat'=4] {'lat'}, use_global_device_ids=true, to_apply=%region_1.2 | all-reduce | flops 10240 | bytes 81920 | tf_op jit(solution)/shard_map/psum | solution.py:53
  49.2 1.0 convolution_add_fusion.2
  50.4 11.7 %cholesky.59 = f32[128,128]{1,0:T(8,128)S(1)} custom-call(f32[128,128]{1,0:T(8,128)S(1)} %fusion.81), custom_call_target="Cholesky" | custom-call | tf_op jit(solution)/shard_map/jit(cholesky)/cholesky | solution.py:24
  62.1 0.7 compare_reduce_fusion.2
  62.8 0.7 fusion.49
  63.6 9.8 %custom-call.16 = f32[1,128,128]{1,2,0:T(8,128)S(1)} custom-call(f32[1,128,128]{2,1,0:T(8,128)S(1)} %fusion.49), custom_call_target="InvertDiagBlocksLowerTriangular" | custom-call | tf_op jit(solution)/shard_map/jit(_cho_solve)/triangular_solve | solution.py:25
  73.4 0.9 fusion.79
  75.0 7.3 %fusion.8 = f32[128,32,256]{2,0,1:T(8,128)} fusion(f32[10,32,8,256]{3,2,1,0:T(8,128)} %bitcast.216, f32[128,256]{1,0:T(8,128)S(1)} %get-tuple-element.13, f32[128,80]{0,1:T(8,128)S(1)} %psum.21, f32[128]{0:T(128)S(1)} %copy-done.9, f32[128]{0:T(128)S(1)} %broadcast_multiply_fusion.4), kind=kOutput, calls=%fused_computation.13 | convolution fusion | flops 1007712256 | bytes 6988800 | tf_op jit(solution)/shard_map/dot_general | solution.py:63
  82.3 5.6 %copy.21 = f32[128,32,256]{0,2,1:T(8,128)} copy(f32[128,32,256]{2,0,1:T(8,128)} %fusion.8) | data formatting | bytes 8388608 | tf_op jit(solution)/shard_map/mul | solution.py:64
  87.9 6.1 %fusion.52 = f32[81,8192]{1,0:T(8,128)S(1)} fusion(f32[128,8192]{0,1:T(8,128)} %bitcast.210, f32[1,128]{0,1:T(8,128)S(1)} %copy.19, f32[80,128]{0,1:T(8,128)S(1)} %fusion.15), kind=kOutput, calls=%fused_computation.92 | convolution fusion | flops 1019226240 | bytes 6889984 | tf_op jit(solution)/shard_map/dot_general | solution.py:67
  94.6 1.3 collective-permute-done.3
  95.9 1.6 collective-permute-start.4
  97.4 4.8 %collective-permute-done.4 = f32[2,80,256]{2,1,0:T(8,128)S(1)} collective-permute-done((f32[2,80,256]{2,1,0:T(8,128)S(1)}, f32[2,80,256]{2,1,0:T(8,128)S(1)}, u32[]{:S(2)}, u32[]{:S(2)}) %collective-permute-start.4) | collective-permute-done | bytes 163872 | tf_op jit(solution)/shard_map/ppermute | solution.py:11
  102.2 1.6 collective-permute-start.5
  104.3 5.2 %copy.35 = f32[16,8,32,256]{3,1,2,0:T(8,128)} copy(f32[16,8,32,256]{3,2,1,0:T(8,128)S(1)} %bitcast.213) | data formatting | bytes 8388608
  109.5 1.7 collective-permute-done.5
  111.2 0.8 convolution_bitcast_fusion.1
  112.0 16.3 %psum.22 = f32[128,80]{0,1:T(8,128)S(1)} all-reduce(f32[128,80]{0,1:T(8,128)S(1)} %convolution_bitcast_fusion.1), channel_id=1, replica_groups=mesh['lon'=8,'lat'=4] {'lat'}, use_global_device_ids=true, to_apply=%region_6.10 | all-reduce | flops 10240 | bytes 81920 | tf_op jit(solution)/shard_map/psum | solution.py:53
  128.7 11.7 %cholesky.70 = f32[128,128]{1,0:T(8,128)S(1)} custom-call(f32[128,128]{1,0:T(8,128)S(1)} %fusion.75), custom_call_target="Cholesky" | custom-call | tf_op jit(solution)/shard_map/jit(cholesky)/cholesky | solution.py:24
  140.5 0.7 compare_reduce_fusion.1
  141.8 9.8 %custom-call.18 = f32[1,128,128]{1,2,0:T(8,128)S(1)} custom-call(f32[1,128,128]{2,1,0:T(8,128)S(1)} %fusion.50), custom_call_target="InvertDiagBlocksLowerTriangular" | custom-call | tf_op jit(solution)/shard_map/jit(_cho_solve)/triangular_solve | solution.py:25
  152.6 5.6 %convolution_multiply_fusion.1 = f32[128,8192]{1,0:T(8,128)S(1)} fusion(f32[128,8192]{1,0:T(8,128)} %bitcast.212, f32[80,8192]{1,0:T(8,128)S(1)} %copy-done.1, f32[8192]{0:T(1024)S(1)} %broadcast_multiply_fusion.1, f32[128,80]{0,1:T(8,128)S(1)} %psum.22, f32[128]{0:T(128)S(1)} %copy-done.8, f32[128]{0:T(128)S(1)} %broadcast_multiply_fusion.3), kind=kOutput, calls=%fused_computation.1 | convolution fusion | flops 1008367616 | bytes 11084800 | tf_op jit(solution)/shard_map/dot_general | solution.py:63
  158.2 3.0 %fusion.56 = f32[81,8192]{1,0:T(8,128)S(1)} fusion(f32[128,8192]{1,0:T(8,128)S(1)} %convolution_multiply_fusion.1, f32[1,128]{0,1:T(8,128)S(1)} %copy.24, f32[80,128]{0,1:T(8,128)S(1)} %fusion.14), kind=kOutput, calls=%fused_computation.96 | convolution fusion | flops 1019226240 | bytes 6889984 | tf_op jit(solution)/shard_map/dot_general | solution.py:67
  161.9 1.3 collective-permute-done.6
  163.2 1.6 collective-permute-start.7
  164.7 4.8 %collective-permute-done.7 = f32[2,80,256]{2,1,0:T(8,128)S(1)} collective-permute-done((f32[2,80,256]{2,1,0:T(8,128)S(1)}, f32[2,80,256]{2,1,0:T(8,128)S(1)}, u32[]{:S(2)}, u32[]{:S(2)}) %collective-permute-start.7) | collective-permute-done | bytes 163872 | tf_op jit(solution)/shard_map/ppermute | solution.py:11
  169.5 1.6 collective-permute-start.8
  171.6 5.2 %copy.36 = f32[16,8,32,256]{3,1,2,0:T(8,128)} copy(f32[16,8,32,256]{3,2,1,0:T(8,128)S(1)} %bitcast.214) | data formatting | bytes 8388608
  176.8 1.7 collective-permute-done.8
  178.5 0.8 convolution_bitcast_fusion
  179.3 18.4 %psum.23 = f32[128,80]{0,1:T(8,128)S(1)} all-reduce(f32[128,80]{0,1:T(8,128)S(1)} %convolution_bitcast_fusion), channel_id=1, replica_groups=mesh['lon'=8,'lat'=4] {'lat'}, use_global_device_ids=true, to_apply=%region_9.13 | all-reduce | flops 10240 | bytes 81920 | tf_op jit(solution)/shard_map/psum | solution.py:53
  198.2 11.7 %cholesky.81 = f32[128,128]{1,0:T(8,128)S(1)} custom-call(f32[128,128]{1,0:T(8,128)S(1)} %fusion.69), custom_call_target="Cholesky" | custom-call | tf_op jit(solution)/shard_map/jit(cholesky)/cholesky | solution.py:24
  209.9 0.6 compare_reduce_fusion
  210.6 0.7 fusion.51
  211.3 9.8 %custom-call.20 = f32[1,128,128]{1,2,0:T(8,128)S(1)} custom-call(f32[1,128,128]{2,1,0:T(8,128)S(1)} %fusion.51), custom_call_target="InvertDiagBlocksLowerTriangular" | custom-call | tf_op jit(solution)/shard_map/jit(_cho_solve)/triangular_solve | solution.py:25
  222.1 5.6 %convolution_multiply_fusion = f32[128,8192]{1,0:T(8,128)S(1)} fusion(f32[128,8192]{1,0:T(8,128)} %bitcast.211, f32[80,8192]{1,0:T(8,128)S(1)} %get-tuple-element.8, f32[8192]{0:T(1024)S(1)} %broadcast_multiply_fusion, f32[128,80]{0,1:T(8,128)S(1)} %psum.23, f32[128]{0:T(128)S(1)} %copy-done.7, f32[128]{0:T(128)S(1)} %broadcast_multiply_fusion.2), kind=kOutput, calls=%fused_computation | convolution fusion | flops 1008367616 | bytes 11084800 | tf_op jit(solution)/shard_map/dot_general | solution.py:63
  227.7 3.2 %fusion.60 = f32[81,8192]{1,0:T(8,128)S(1)} fusion(f32[128,8192]{1,0:T(8,128)S(1)} %convolution_multiply_fusion, f32[1,128]{0,1:T(8,128)S(1)} %copy.27, f32[80,128]{0,1:T(8,128)S(1)} %fusion.13), kind=kOutput, calls=%fused_computation.100 | convolution fusion | flops 1019226240 | bytes 6889984 | tf_op jit(solution)/shard_map/dot_general | solution.py:67
  231.4 2.3 copy.37
  (97 shorter events, 10.1 us)
Async XLA Ops:
  0.0 4.0 %copy-start.12 = (s32[3,128]{1,0:T(4,128)S(1)}, s32[3,128]{1,0:T(4,128)}, u32[]{:S(2)}) copy-start(s32[3,128]{1,0:T(4,128)} %param.12) | copy-start | bytes 4612
  0.0 4.0 %copy-start.13 = (s32[3,128]{1,0:T(4,128)S(1)}, s32[3,128]{1,0:T(4,128)}, u32[]{:S(2)}) copy-start(s32[3,128]{1,0:T(4,128)} %param.13) | copy-start | bytes 4612
  3.4 5.5 %collective-permute-start = (f32[1,80,256]{2,1,0:T(8,128)S(1)}, f32[1,80,256]{2,1,0:T(8,128)S(1)}, u32[]{:S(2)}, u32[]{:S(2)}) collective-permute-start(f32[1,80,256]{2,1,0:T(8,128)S(1)} %slice_bitcast_fusion.2), channel_id=1, source_target_pairs={{0,4},{4,0},{8,12},{12,8},{16,20},{20,16},{24,28},{28,24},{1,5},{5... | collective-permute-start | bytes 245768 | tf_op jit(solution)/shard_map/ppermute | solution.py:11
  7.2 11.7 %copy-start.5 = (f32[3,128]{1,0:T(4,128)S(1)}, f32[3,128]{1,0:T(4,128)}, u32[]{:S(2)}) copy-start(f32[3,128]{1,0:T(4,128)} %param.15) | copy-start | bytes 4612
  7.2 12.9 %copy-start.3 = (s32[1,1,3,128,256]{4,3,2,1,0:T(8,128)S(1)}, s32[1,1,3,128,256]{4,3,2,1,0:T(8,128)}, u32[]{:S(2)}) copy-start(s32[1,1,3,128,256]{4,3,2,1,0:T(8,128)} %param.16) | copy-start | bytes 1179652
  9.0 65.5 %copy-start.6 = (f32[3,128]{1,0:T(4,128)S(1)}, f32[3,128]{1,0:T(4,128)}, u32[]{:S(2)}) copy-start(f32[3,128]{1,0:T(4,128)} %param.14) | copy-start | bytes 4612
  9.0 7.4 %collective-permute-start.1 = (f32[2,80,256]{2,1,0:T(8,128)S(1)}, f32[2,80,256]{2,1,0:T(8,128)S(1)}, u32[]{:S(2)}, u32[]{:S(2)}) collective-permute-start(f32[2,80,256]{2,1,0:T(8,128)S(1)} %maximum_select_fusion.9), channel_id=1, source_target_pairs={{0,8},{4,12},{8,0},{12,4},{16,24},{20,28},{24,16},{28,20},{1,9},{5... | collective-permute-start | bytes 491528 | tf_op jit(solution)/shard_map/ppermute | solution.py:11
  17.1 9.8 %collective-permute-start.2 = (f32[4,80,256]{2,1,0:T(8,128)}, f32[4,80,256]{2,1,0:T(8,128)}, u32[]{:S(2)}, u32[]{:S(2)}) collective-permute-start(f32[4,80,256]{2,1,0:T(8,128)} %maximum_select_fusion.6), channel_id=1, source_target_pairs={{0,16},{4,20},{8,24},{12,28},{16,0},{20,4},{24,8},{28,12},{1,17},{... | collective-permute-start | bytes 983048 | tf_op jit(solution)/shard_map/ppermute | solution.py:11
  20.2 54.9 %copy-start.9 = (f32[128]{0:T(128)S(1)}, f32[128]{0:T(128)}, u32[]{:S(2)}) copy-start(f32[128]{0:T(128)} %get-tuple-element.18) | copy-start | bytes 1540
  87.9 6.1 %copy-start.4 = (f32[1,1,32,256]{3,1,2,0:T(1,128)S(1)}, f32[1,1,32,256]{3,1,2,0:T(1,128)}, u32[]{:S(2)}) copy-start(f32[1,1,32,256]{3,1,2,0:T(1,128)} %copy.34) | copy-start | bytes 98308
  94.0 9.8 %copy-start.11 = (s32[128]{0:T(128)S(1)}, s32[128]{0:T(128)}, u32[]{:S(2)}) copy-start(s32[128]{0:T(128)} %get-tuple-element.25) | copy-start | bytes 1540
  94.5 9.8 %copy-start = (f32[80,8192]{1,0:T(8,128)}, f32[80,8192]{1,0:T(8,128)S(1)}, u32[]{:S(2)}) copy-start(f32[80,8192]{1,0:T(8,128)S(1)} %get-tuple-element.11) | copy-start | bytes 7864324
  94.5 1.3 collective-permute-start.3
  95.9 6.3 %collective-permute-start.4 = (f32[2,80,256]{2,1,0:T(8,128)S(1)}, f32[2,80,256]{2,1,0:T(8,128)S(1)}, u32[]{:S(2)}, u32[]{:S(2)}) collective-permute-start(f32[2,80,256]{2,1,0:T(8,128)S(1)} %maximum_select_fusion.10), channel_id=1, source_target_pairs={{0,8},{4,12},{8,0},{12,4},{16,24},{20,28},{24,16},{28,20},{1,9},{5... | collective-permute-start | bytes 491528 | tf_op jit(solution)/shard_map/ppermute | solution.py:11
  102.2 9.0 %collective-permute-start.5 = (f32[4,80,256]{2,1,0:T(8,128)S(1)}, f32[4,80,256]{2,1,0:T(8,128)S(1)}, u32[]{:S(2)}, u32[]{:S(2)}) collective-permute-start(f32[4,80,256]{2,1,0:T(8,128)S(1)} %maximum_select_fusion.7), channel_id=1, source_target_pairs={{0,16},{4,20},{8,24},{12,28},{16,0},{20,4},{24,8},{28,12},{1,17},{... | collective-permute-start | bytes 983048 | tf_op jit(solution)/shard_map/ppermute | solution.py:11
  104.2 7.0 %copy-start.15 = (pred[128,8]{0,1:T(8,128)(4,1)S(1)}, pred[128,8]{0,1:T(8,128)(4,1)}, u32[]{:S(2)}) copy-start(pred[128,8]{0,1:T(8,128)(4,1)} %get-tuple-element.27) | copy-start | bytes 3076
  104.3 24.1 %copy-start.8 = (f32[128]{0:T(128)S(1)}, f32[128]{0:T(128)}, u32[]{:S(2)}) copy-start(f32[128]{0:T(128)} %get-tuple-element.19) | copy-start | bytes 1540
  109.5 43.1 %copy-start.1 = (f32[80,8192]{1,0:T(8,128)S(1)}, f32[80,8192]{1,0:T(8,128)}, u32[]{:S(2)}) copy-start(f32[80,8192]{1,0:T(8,128)} %copy-done) | copy-start | bytes 7864324
  158.2 3.1 %copy-start.2 = (f32[80,8192]{1,0:T(8,128)S(1)}, f32[80,8192]{1,0:T(8,128)}, u32[]{:S(2)}) copy-start(f32[80,8192]{1,0:T(8,128)} %copy-done) | copy-start | bytes 7864324
  161.3 9.8 %copy-start.10 = (s32[128]{0:T(128)S(1)}, s32[128]{0:T(128)}, u32[]{:S(2)}) copy-start(s32[128]{0:T(128)} %get-tuple-element.23) | copy-start | bytes 1540
  161.8 1.3 collective-permute-start.6
  163.2 6.3 %collective-permute-start.7 = (f32[2,80,256]{2,1,0:T(8,128)S(1)}, f32[2,80,256]{2,1,0:T(8,128)S(1)}, u32[]{:S(2)}, u32[]{:S(2)}) collective-permute-start(f32[2,80,256]{2,1,0:T(8,128)S(1)} %maximum_select_fusion.11), channel_id=1, source_target_pairs={{0,8},{4,12},{8,0},{12,4},{16,24},{20,28},{24,16},{28,20},{1,9},{5... | collective-permute-start | bytes 491528 | tf_op jit(solution)/shard_map/ppermute | solution.py:11
  169.5 9.0 %collective-permute-start.8 = (f32[4,80,256]{2,1,0:T(8,128)S(1)}, f32[4,80,256]{2,1,0:T(8,128)S(1)}, u32[]{:S(2)}, u32[]{:S(2)}) collective-permute-start(f32[4,80,256]{2,1,0:T(8,128)S(1)} %maximum_select_fusion.8), channel_id=1, source_target_pairs={{0,16},{4,20},{8,24},{12,28},{16,0},{20,4},{24,8},{28,12},{1,17},{... | collective-permute-start | bytes 983048 | tf_op jit(solution)/shard_map/ppermute | solution.py:11
  171.6 7.0 %copy-start.14 = (pred[128,8]{0,1:T(8,128)(4,1)S(1)}, pred[128,8]{0,1:T(8,128)(4,1)}, u32[]{:S(2)}) copy-start(pred[128,8]{0,1:T(8,128)(4,1)} %get-tuple-element.26) | copy-start | bytes 3076
  171.6 26.2 %copy-start.7 = (f32[128]{0:T(128)S(1)}, f32[128]{0:T(128)}, u32[]{:S(2)}) copy-start(f32[128]{0:T(128)} %get-tuple-element.17) | copy-start | bytes 1540
